TPU v7x, 32 devices: a whole 2x2x4 slice. The times are simulated.
32 devices in a mesh: shard: 2 (over x), ctx: 4 (over y, core), tp: 4 (over z).
Axes of the slice: x: 2, y: 2, z: 4, core: 2. Of those that a mesh axis runs over, the one named last changes fastest.
Arguments:
- tokens: bfloat16 [8, 1024, 767], P('shard', 'ctx'), may hold values from -6 to 6
- lengths: int32 [8], P('shard'), may hold values from 256 to 1024, as said below
- first_gain: float32 [768], replicated, may hold values from 0.5 to 1.5
- entry_weight: bfloat16 [3, 768, 768], P(None, ('shard', 'ctx'), 'tp'), may hold values from -0.21875 to 0.21875
- entry_bias: float32 [2, 768], P(None, 'tp'), may hold values from -3 to 3
- exit_weight: bfloat16 [768, 768], P('tp', ('shard', 'ctx')), may hold values from -0.625 to 0.625
- exit_bias: float32 [768], replicated, may hold values from -3 to 3
- second_gain: float32 [768], replicated, may hold values from 0.5 to 1.5
- hidden_weight: bfloat16 [768, 3072], P(('shard', 'ctx'), 'tp'), may hold values from -0.21875 to 0.21875
- hidden_bias: float32 [3072], P('tp'), may hold values from -3 to 3
- return_weight: bfloat16 [3072, 768], P('tp', ('shard', 'ctx')), may hold values from -0.109375 to 0.109375
- return_bias: float32 [768], replicated, may hold values from -3 to 3
- cotangent: bfloat16 [8, 1024, 767], P('shard', 'ctx'), may hold values from -6 to 6
Outputs:
- result: bfloat16 [8, 1024, 767], P('shard', 'ctx')
- tokens_gradient: bfloat16 [8, 1024, 767], P('shard', 'ctx')
- first_gain_gradient: float32 [768], replicated
- entry_weight_gradient: float32 [3, 768, 768], P(None, ('shard', 'ctx'), 'tp')
- entry_bias_gradient: float32 [2, 768], P(None, 'tp')
- exit_weight_gradient: float32 [768, 768], P('tp', ('shard', 'ctx'))
- exit_bias_gradient: float32 [768], replicated
- second_gain_gradient: float32 [768], replicated
- hidden_weight_gradient: float32 [768, 3072], P(('shard', 'ctx'), 'tp')
- hidden_bias_gradient: float32 [3072], P('tp')
- return_weight_gradient: float32 [3072, 768], P('tp', ('shard', 'ctx'))
- return_bias_gradient: float32 [768], replicated
Inputs may be any that keep to these rules, and one draw needn't show every extreme that they name: `lengths`: in every draw some sequence has exactly 1024 valid positions and some has exactly 256.
All inputs are finite; a program needn't handle non-finite values.
Results may differ from a plain program's by a relative error of at most 0.014.
Values may be sent and summed in bfloat16 or wider, within the bound.
No kernel may reach another device: no remote copies, remote signals or barrier semaphores. Data moves between devices by JAX's collectives and lax.ppermute only.
A program may use at most 256 MiB of HBM per device.

v0:
```python
import math
import jax
import jax.numpy as jnp
from jax import lax
from jax.sharding import PartitionSpec as P

HDIM = 64
EPSILON = 1e-05


def row_mean(values):
    return jnp.mean(values, -1, keepdims=True)


def shards(
    tokens,
    lengths,
    first_gain,
    entry_weight,
    entry_bias,
    exit_weight,
    exit_bias,
    second_gain,
    hidden_weight,
    hidden_bias,
    return_weight,
    return_bias,
    cotangent,
):
    seq_dev, local, narrow = tokens.shape
    row_count = seq_dev * local
    full_len = local * lax.axis_size("ctx")
    head_width = entry_weight.shape[2]
    heads_here = head_width // HDIM
    scale = 1.0 / math.sqrt(HDIM)
    bfloat = jnp.bfloat16
    single = jnp.float32
    full_entry, full_exit, full_hidden, full_return = (
        lax.all_gather(entry_weight, ("shard", "ctx"), axis=1, tiled=True),
        lax.all_gather(exit_weight, ("shard", "ctx"), axis=1, tiled=True),
        lax.all_gather(hidden_weight, ("shard", "ctx"), axis=0, tiled=True),
        lax.all_gather(return_weight, ("shard", "ctx"), axis=1, tiled=True),
    )
    stream_part = tokens.astype(single).reshape(row_count, narrow)
    stream = jnp.concatenate([stream_part, -jnp.sum(stream_part, -1, keepdims=True)], 1)
    first_inverse = lax.rsqrt(row_mean(stream * stream) + EPSILON)
    first_unit = stream * first_inverse
    first_normed = (first_unit * first_gain).astype(bfloat)
    queries = (
        jnp.dot(first_normed, full_entry[0], preferred_element_type=single) + entry_bias[0]
    ).astype(bfloat)
    keys = jnp.dot(first_normed, full_entry[1], preferred_element_type=single).astype(bfloat)
    values = (
        jnp.dot(first_normed, full_entry[2], preferred_element_type=single) + entry_bias[1]
    ).astype(bfloat)
    seq_shape = (seq_dev, local, head_width)
    all_keys, all_values = (
        lax.all_gather(keys.reshape(seq_shape), "ctx", axis=1, tiled=True),
        lax.all_gather(values.reshape(seq_shape), "ctx", axis=1, tiled=True),
    )
    offset = lax.axis_index("ctx") * local
    query_pos = offset + jnp.arange(local, dtype=jnp.int32)
    key_pos = jnp.arange(full_len, dtype=jnp.int32)
    local_heads = (seq_dev, local, heads_here, HDIM)
    full_heads = (seq_dev, full_len, heads_here, HDIM)
    allowed = (
        (key_pos[None, None, :] <= query_pos[None, :, None])
        & (key_pos[None, None, :] < lengths[:, None, None])
    )[:, None]

    def masked_scores(query_block, key_block):
        raw_scores = (
            jnp.einsum("sqhd,skhd->shqk", query_block, key_block, preferred_element_type=single)
            * scale
        )
        return jnp.where(allowed, raw_scores, -1e30)

    query_heads = queries.reshape(local_heads)
    scores = masked_scores(query_heads, all_keys.reshape(full_heads))
    largest = jnp.max(scores, -1, keepdims=True)
    exponent = jnp.exp(scores - largest)
    totals = jnp.sum(exponent, -1, keepdims=True)
    weights = (exponent / totals).astype(bfloat)
    log_totals = largest + jnp.log(totals)
    attended = jnp.einsum(
        "shqk,skhd->sqhd", weights, all_values.reshape(full_heads), preferred_element_type=single
    ).astype(bfloat)
    attended_rows = attended.reshape(row_count, head_width)
    exit_term = jnp.dot(attended_rows, full_exit, preferred_element_type=single)
    branch = lax.psum(exit_term, "tp") + exit_bias
    middle = stream + branch - row_mean(branch)
    second_inverse = lax.rsqrt(row_mean(middle * middle) + EPSILON)
    second_unit = middle * second_inverse
    second_normed = (second_unit * second_gain).astype(bfloat)
    hidden = jnp.dot(second_normed, full_hidden, preferred_element_type=single) + hidden_bias
    activated, gelu_pull = jax.vjp(
        lambda values_in: jax.nn.gelu(values_in, approximate=True), hidden
    )
    activated_low = activated.astype(bfloat)
    return_term = jnp.dot(activated_low, full_return, preferred_element_type=single)
    returned = lax.psum(return_term.astype(jnp.bfloat16), "tp").astype(jnp.float32) + return_bias
    full_stream = middle + returned - row_mean(returned)
    result_rows = full_stream[:, :narrow].astype(bfloat)
    result = result_rows.reshape(seq_dev, local, narrow)
    full_entry, full_exit, full_hidden, full_return = (
        lax.all_gather(entry_weight, ("shard", "ctx"), axis=1, tiled=True),
        lax.all_gather(exit_weight, ("shard", "ctx"), axis=1, tiled=True),
        lax.all_gather(hidden_weight, ("shard", "ctx"), axis=0, tiled=True),
        lax.all_gather(return_weight, ("shard", "ctx"), axis=1, tiled=True),
    )
    valid = (query_pos[None, :] < lengths[:, None]).astype(single).reshape(row_count, 1)
    cot_rows = cotangent.astype(single).reshape(row_count, narrow) * valid
    cot_full = jnp.concatenate([cot_rows, jnp.zeros((row_count, 1), single)], 1)
    returned_grad = (cot_full - row_mean(cot_full)).astype(bfloat)
    return_bias_grad = jnp.sum(returned_grad.astype(single), 0)
    return_weight_grad = jnp.einsum(
        "rf,rd->fd", activated_low, returned_grad, preferred_element_type=single
    )
    activated_grad = jnp.einsum(
        "rd,fd->rf", returned_grad, full_return, preferred_element_type=single
    )
    hidden_grad = gelu_pull(activated_grad)[0].astype(bfloat)
    hidden_bias_grad = jnp.sum(hidden_grad.astype(single), 0)
    hidden_weight_grad = jnp.einsum(
        "rd,rf->df", second_normed, hidden_grad, preferred_element_type=single
    )
    second_term = jnp.einsum("rf,df->rd", hidden_grad, full_hidden, preferred_element_type=single)
    second_grad = lax.psum(second_term, "tp")
    second_gain_grad = jnp.sum(second_grad * second_unit, 0)
    second_scaled = second_grad * second_gain
    middle_grad = cot_full + second_inverse * (
        second_scaled - second_unit * row_mean(second_scaled * second_unit)
    )
    branch_grad = (middle_grad - row_mean(middle_grad)).astype(bfloat)
    exit_bias_grad = jnp.sum(branch_grad.astype(single), 0)
    exit_weight_grad = jnp.einsum(
        "re,rd->ed", attended_rows, branch_grad, preferred_element_type=single
    )
    attended_grad = jnp.einsum(
        "rd,ed->re", branch_grad, full_exit, preferred_element_type=single
    ).astype(bfloat)
    all_keys, all_values = (
        lax.all_gather(keys.reshape(seq_shape), "ctx", axis=1, tiled=True),
        lax.all_gather(values.reshape(seq_shape), "ctx", axis=1, tiled=True),
    )
    key_heads = all_keys.reshape(full_heads)
    value_heads = all_values.reshape(full_heads)
    out_grad = attended_grad.reshape(local_heads)
    back_scores = masked_scores(query_heads, key_heads)
    probs = jnp.exp(back_scores - log_totals)
    probs_low = probs.astype(bfloat)
    prob_rounded = lax.optimization_barrier(
        jnp.einsum("sqhd,skhd->shqk", out_grad, value_heads, preferred_element_type=single).astype(
            bfloat
        )
    )
    prob_grad = prob_rounded.astype(single)
    inner = jnp.sum(probs * prob_grad, -1, keepdims=True)
    score_grad = (probs * (prob_grad - inner)).astype(bfloat)
    query_grads = (
        jnp.einsum("shqk,skhd->sqhd", score_grad, key_heads, preferred_element_type=single) * scale
    ).astype(bfloat)
    key_parts = (
        jnp.einsum("shqk,sqhd->skhd", score_grad, query_heads, preferred_element_type=single)
        * scale
    )
    value_parts = jnp.einsum("shqk,sqhd->skhd", probs_low, out_grad, preferred_element_type=single)
    key_sums, value_sums = (
        lax.psum_scatter(
            key_parts.reshape(seq_dev, full_len, head_width), "ctx", scatter_dimension=1, tiled=True
        ),
        lax.psum_scatter(
            value_parts.reshape(seq_dev, full_len, head_width),
            "ctx",
            scatter_dimension=1,
            tiled=True,
        ),
    )
    query_low = query_grads.reshape(row_count, head_width)
    key_low = key_sums.reshape(row_count, head_width).astype(bfloat)
    value_low = value_sums.reshape(row_count, head_width).astype(bfloat)
    entry_bias_grad = jnp.stack(
        [jnp.sum(query_low.astype(single), 0), jnp.sum(value_low.astype(single), 0)]
    )
    entry_weight_grad = jnp.stack(
        [
            jnp.einsum("rd,re->de", first_normed, query_low, preferred_element_type=single),
            jnp.einsum("rd,re->de", first_normed, key_low, preferred_element_type=single),
            jnp.einsum("rd,re->de", first_normed, value_low, preferred_element_type=single),
        ]
    )
    first_part = (
        jnp.einsum("re,de->rd", query_low, full_entry[0], preferred_element_type=single)
        + jnp.einsum("re,de->rd", key_low, full_entry[1], preferred_element_type=single)
        + jnp.einsum("re,de->rd", value_low, full_entry[2], preferred_element_type=single)
    )
    first_grad = lax.psum(first_part, "tp")
    first_gain_grad = jnp.sum(first_grad * first_unit, 0)
    first_scaled = first_grad * first_gain
    stream_grad = middle_grad + first_inverse * (
        first_scaled - first_unit * row_mean(first_scaled * first_unit)
    )
    tokens_rows = (stream_grad[:, :narrow] - stream_grad[:, narrow:]).astype(bfloat)
    tokens_grad = tokens_rows.reshape(seq_dev, local, narrow)
    weight_grads = (
        lax.psum_scatter(entry_weight_grad, ("shard", "ctx"), scatter_dimension=1, tiled=True),
        lax.psum_scatter(exit_weight_grad, ("shard", "ctx"), scatter_dimension=1, tiled=True),
        lax.psum_scatter(hidden_weight_grad, ("shard", "ctx"), scatter_dimension=0, tiled=True),
        lax.psum_scatter(return_weight_grad, ("shard", "ctx"), scatter_dimension=1, tiled=True),
    )
    small_grads = lax.psum(
        (
            first_gain_grad,
            entry_bias_grad,
            exit_bias_grad,
            second_gain_grad,
            hidden_bias_grad,
            return_bias_grad,
        ),
        ("shard", "ctx"),
    )
    return (
        result,
        tokens_grad,
        small_grads[0],
        weight_grads[0],
        small_grads[1],
        weight_grads[1],
        small_grads[2],
        small_grads[3],
        weight_grads[2],
        small_grads[4],
        weight_grads[3],
        small_grads[5],
    )


def solution(mesh):
    return jax.shard_map(
        shards,
        mesh=mesh,
        in_specs=(
            P("shard", "ctx", None),
            P("shard"),
            P(),
            P(None, ("shard", "ctx"), "tp"),
            P(None, "tp"),
            P("tp", ("shard", "ctx")),
            P(),
            P(),
            P(("shard", "ctx"), "tp"),
            P("tp"),
            P("tp", ("shard", "ctx")),
            P(),
            P("shard", "ctx", None),
        ),
        out_specs=(
            P("shard", "ctx", None),
            P("shard", "ctx", None),
            P(),
            P(None, ("shard", "ctx"), "tp"),
            P(None, "tp"),
            P("tp", ("shard", "ctx")),
            P(),
            P(),
            P(("shard", "ctx"), "tp"),
            P("tp"),
            P("tp", ("shard", "ctx")),
            P(),
        ),
        check_vma=False,
    )
```

profile of v0, /device:TPU:0, one launch (start us, length us, event | category | flops | bytes accessed | tf_op | source)
XLA Modules:
  0.0 1059.9 jit_solution(7665863335763462059)
XLA Ops:
  8.1 2.3 convert_reduce_fusion.5
  10.3 2.9 copy.52
  14.5 13.1 %all_gather.24 = bf16[3,768,192]{2,1,0:T(8,128)(2,1)S(1)} all-gather(bf16[3,96,192]{2,1,0:T(8,128)(2,1)S(1)} %copy-done.38), channel_id=1, replica_groups=mesh['shard'=2,'ctx'=4,'tp'=4] {'shard','ctx'}, dimensions={1}, use_global_device_ids=true | all-gather | bytes 995328 | tf_op jit(solution)/shard_map/all_gather | solution.py:39
  27.7 1.8 multiply_reduce_fusion.5
  33.1 2.1 fusion.20
  36.3 2.9 fusion.21
  39.2 1.5 copy.58
  42.1 12.4 %all_gather.27 = bf16[192,768]{0,1:T(8,128)(2,1)} all-gather(bf16[192,96]{0,1:T(8,128)(2,1)} %copy.58), channel_id=1, replica_groups=mesh['shard'=2,'ctx'=4,'tp'=4] {'shard','ctx'}, dimensions={1}, use_global_device_ids=true | all-gather | bytes 331776 | tf_op jit(solution)/shard_map/all_gather | solution.py:40
  55.2 1.4 broadcast_and_fusion
  56.7 2.0 copy.55
  58.6 2.9 fusion.38
  61.6 4.6 copy-done
  66.2 3.4 fusion.3
  69.6 6.6 all-gather.5.cloned.1.call-done
  76.2 1.9 copy.54
  78.1 6.6 fusion.24
  85.8 2.2 fusion.39
  89.6 4.3 copy.59
  94.0 2.2 bitcast_multiply_fusion
  96.4 1.4 copy-done.8
  97.9 2.1 convert_reduce_fusion
  99.9 109.4 %all-reduce.7.cloned.1.call-done = f32[1024,768]{1,0:T(8,128)} async-done(((f32[1024,768]{1,0:T(8,128)}), f32[1024,768]{1,0:T(8,128)}) %all-reduce.7.cloned.1.call-update) | async-done | bytes 3145744 | tf_op jit(solution)/shard_map/psum | solution.py:90
  209.3 2.2 add_reduce_fusion
  211.6 4.3 multiply_reduce_fusion.4
  215.9 5.5 fusion.33
  221.4 5.6 convert_reduce_fusion.1
  228.2 3.1 fusion.40
  232.5 119.0 %all-reduce.11.cloned.1.call-done = f32[1024,768]{1,0:T(8,128)} async-done(((f32[1024,768]{1,0:T(8,128)}), f32[1024,768]{1,0:T(8,128)}) %all-reduce.11.cloned.1.call-update) | async-done | bytes 3145744 | tf_op jit(solution)/shard_map/psum | solution.py:128
  351.5 3.5 multiply_reduce_fusion
  356.8 1.7 copy-done.10
  361.6 1.8 convolution_convert_fusion
  363.4 7.6 fusion
  371.1 3.0 fusion.2
  376.7 48.2 %copy.69 = f32[4,1024,192]{0,2,1:T(8,128)} copy(f32[4,1024,192]{1,2,0:T(8,128)S(1)} %bitcast.133) | data formatting | bytes 6291456
  424.9 84.3 %reshape.241 = f32[1024,768]{1,0:T(8,128)} reshape(f32[1024,192,4]{2,1,0:T(8,128)} %bitcast.22) | data formatting | bytes 6291456
  509.8 6.3 fusion.5
  516.1 48.3 %copy.71 = f32[4,1024,192]{0,2,1:T(8,128)} copy(f32[4,1024,192]{1,2,0:T(8,128)S(1)} %bitcast.127) | data formatting | bytes 6291456
  564.3 84.3 %reshape.243 = f32[1024,768]{1,0:T(8,128)} reshape(f32[1024,192,4]{2,1,0:T(8,128)} %bitcast.25) | data formatting | bytes 6291456
  649.9 5.1 convolution_convert_fusion.1
  655.2 1.6 convolution_bitcast_fusion
  657.0 5.1 convert_reduce_fusion.4
  663.8 29.2 %reshape.242 = bf16[256,192,4]{2,1,0:T(8,128)(2,1)} reshape(f32[256,768]{1,0:T(8,128)} %reduce-scatter.19.cloned.1.call-done) | data formatting | bytes 1179648
  693.0 12.2 %copy.70 = bf16[4,256,192]{1,0,2:T(4,128)(2,1)S(1)} copy(bf16[4,256,192]{0,2,1:T(8,128)(2,1)} %bitcast.123) | data formatting | bytes 786432
  705.3 29.3 %reshape.244 = bf16[256,192,4]{2,1,0:T(8,128)(2,1)} reshape(f32[256,768]{1,0:T(8,128)} %reduce-scatter.21.cloned.1.call-done) | data formatting | bytes 1179648
  734.6 12.2 %copy.72 = bf16[4,256,192]{1,0,2:T(4,128)(2,1)S(1)} copy(bf16[4,256,192]{0,2,1:T(8,128)(2,1)} %bitcast.124) | data formatting | bytes 786432
  749.3 2.9 copy.73
  752.2 2.9 reshape.245
  755.4 1.9 fusion.26
  757.9 2.3 add_add_fusion
  760.4 5.8 fusion.34
  766.3 4.4 fusion.32
  770.8 1.8 fusion.25
  772.6 1.5 fusion.18
  774.1 3.9 copy.66
  778.1 15.8 %reduce-scatter.25.cloned.1.call-done = f32[96,192]{1,0:T(8,128)} async-done(((f32[768,192]{1,0:T(8,128)}), f32[96,192]{1,0:T(8,128)}) %reduce-scatter.25.cloned.1.call-update) | async-done | bytes 73744
  793.9 1.6 copy.76
  796.5 40.9 %reduce-scatter.23.cloned.1.call-done = f32[96,576]{1,0:T(8,128)} async-done(((f32[768,576]{1,0:T(8,128)}), f32[96,576]{1,0:T(8,128)}) %reduce-scatter.23.cloned.1.call-update) | async-done | bytes 221200
  839.3 121.4 %all-reduce.13.cloned.1.call-done = f32[1024,768]{1,0:T(8,128)} async-done(((f32[1024,768]{1,0:T(8,128)}), f32[1024,768]{1,0:T(8,128)}) %all-reduce.13.cloned.1.call-update) | async-done | bytes 3145744 | tf_op jit(solution)/shard_map/psum | solution.py:197
  960.8 3.0 multiply_reduce_fusion.1
  964.9 1.5 multiply_add_fusion
  967.0 2.2 copy.67
  969.2 25.0 %all-reduce.1 = (f32[768]{0:T(1024)}, f32[2,192]{1,0:T(2,128)}, f32[768]{0:T(1024)}, f32[768]{0:T(1024)}, f32[768]{0:T(1024)}, /*index=5*/f32[768]{0:T(1024)}) all-reduce(f32[768]{0:T(1024)S(1)} %get-tuple-element.48, f32[2,192]{1,0:T(2,128)S(1)} %pad_maximum_fusion.2, ...), channel_id=1, replica_groups=mesh['shard'=2,'ctx'=4,'tp'=4] {'shard','ctx'}, use_global_device_ids=true, to_apply=%region_19.20 | all-reduce | flops 4224 | bytes 33792 | tf_op jit(solution)/shard_map/psum | solution.py:211
  994.2 11.9 %reduce-scatter.17.cloned.1.call-done = f32[768,96]{0,1:T(8,128)} async-done(((f32[768,768]{0,1:T(8,128)}), f32[768,96]{0,1:T(8,128)}) %reduce-scatter.17.cloned.1.call-update) | async-done | bytes 294928 | tf_op jit(solution)/shard_map/reduce_scatter | solution.py:209
  1006.1 46.2 %reduce-scatter.15.cloned.1.call-done = f32[96,768]{1,0:T(8,128)} async-done(((f32[768,768]{1,0:T(8,128)}), f32[96,768]{1,0:T(8,128)}) %reduce-scatter.15.cloned.1.call-update) | async-done | bytes 294928 | tf_op jit(solution)/shard_map/reduce_scatter | solution.py:208
  (217 shorter events, 32.6 us)
Async XLA Ops:
  8.0 6.5 copy-start.38
  8.0 48.6 %all-gather.7.cloned.1.call-start = ((), (), s32[]{:S(2)}) async-start(), calls=%async_computation.7 | async-start | bytes 1966080 | tf_op jit(solution)/shard_map/all_gather | solution.py:58
  13.3 198.3 %copy-start.1 = (f32[4,256,767]{2,1,0:T(8,128)}, f32[4,256,767]{2,1,0:T(8,128)S(1)}, u32[]{:S(2)}) copy-start(f32[4,256,767]{2,1,0:T(8,128)S(1)} %copy.52) | copy-start | bytes 9424900
  13.3 16.2 %copy-start.45 = (f32[768]{0:T(1024)S(1)}, f32[768]{0:T(1024)}, u32[]{:S(2)}) copy-start(f32[768]{0:T(1024)} %param.15) | copy-start | bytes 9220
  14.5 15.0 %copy-start.14 = (f32[1,1024]{0,1:T(8,128)S(1)}, f32[1,1024]{0,1:T(8,128)}, u32[]{:S(2)}) copy-start(f32[1,1024]{0,1:T(8,128)} %copy.81) | copy-start | bytes 12292
  29.5 3.5 copy-start.58
  33.0 43.2 %all-gather.5.cloned.1.call-start = ((), (), s32[]{:S(2)}) async-start(), calls=%async_computation.6 | async-start | bytes 1966080 | tf_op jit(solution)/shard_map/all_gather | solution.py:59
  33.1 21.4 %copy-start.59 = (s32[4]{0:T(128)S(1)}, s32[4]{0:T(128)}, u32[]{:S(2)}) copy-start(s32[4]{0:T(128)} %param.14) | copy-start | bytes 52
  36.3 173.0 %all-reduce.7.cloned.1.call-start = ((), (), s32[]{:S(2)}) async-start(), calls=%async_computation.8 | async-start | bytes 6291456 | tf_op jit(solution)/shard_map/psum | solution.py:90
  42.0 19.5 %copy-start.26 = (bf16[4,256,3,64]{1,0,3,2:T(4,128)(2,1)}, bf16[4,256,3,64]{1,0,3,2:T(4,128)(2,1)S(1)}, u32[]{:S(2)}) copy-start(bf16[4,256,3,64]{1,0,3,2:T(4,128)(2,1)S(1)} %reshape.226) | copy-start | bytes 1179652
  58.6 2.9 copy-start.12
  61.5 4.7 copy-start
  61.5 16.6 %copy-start.37 = (f32[4,3,256]{2,1,0:T(4,128)}, f32[4,3,256]{2,1,0:T(4,128)S(1)}, u32[]{:S(2)}) copy-start(f32[4,3,256]{2,1,0:T(4,128)S(1)} %get-tuple-element.72) | copy-start | bytes 36868
  78.1 6.6 copy-start.23
  78.1 7.7 copy-start.30
  85.8 3.7 copy-start.56
  85.8 3.7 copy-start.60
  88.1 127.8 %all-gather.9.cloned.1.call-start = ((), (), s32[]{:S(2)}) async-start(), calls=%async_computation.9 | async-start | bytes 1327104 | tf_op jit(solution)/shard_map/all_gather | solution.py:41
  88.7 132.7 %all-gather.11.cloned.1.call-start = ((), (), s32[]{:S(2)}) async-start(), calls=%async_computation.10 | async-start | bytes 1327104 | tf_op jit(solution)/shard_map/all_gather | solution.py:42
  89.3 262.2 %all-reduce.11.cloned.1.call-start = ((), (), s32[]{:S(2)}) async-start(), calls=%async_computation.12 | async-start | bytes 6291456 | tf_op jit(solution)/shard_map/psum | solution.py:128
  96.4 112.9 %copy-start.47 = (f32[768]{0:T(1024)S(1)}, f32[768]{0:T(1024)}, u32[]{:S(2)}) copy-start(f32[768]{0:T(1024)} %param.19) | copy-start | bytes 9220
  211.6 4.3 copy-start.48
  215.9 5.5 copy-start.42
  215.9 5.5 copy-start.36
  215.9 5.5 copy-start.63
  221.4 6.8 copy-start.62
  231.2 120.2 %copy-start.6 = (f32[1024,768]{1,0:T(8,128)S(1)}, f32[1024,768]{1,0:T(8,128)}, u32[]{:S(2)}) copy-start(f32[1024,768]{1,0:T(8,128)} %get-tuple-element.67) | copy-start | bytes 9437188
  231.3 432.5 %reduce-scatter.19.cloned.1.call-start = ((), (), s32[]{:S(2)}) async-start(), calls=%async_computation.16 | async-start | bytes 3932160
  351.5 3.5 copy-start.9
  351.5 3.8 copy-start.19
  351.5 3.8 copy-start.43
  351.5 3.8 copy-start.49
  358.4 3.1 copy-start.24
  361.6 9.5 slice-start
  361.6 9.5 slice-start.1
  363.4 7.6 slice-start.2
  371.1 3.0 copy-start.27
  374.1 2.6 copy-start.3
  509.3 196.1 %reduce-scatter.21.cloned.1.call-start = ((), (), s32[]{:S(2)}) async-start(), calls=%async_computation.17 | async-start | bytes 3932160
  648.7 6.4 copy-start.18
  648.7 6.4 copy-start.35
  648.7 122.0 %all-reduce.9.cloned.1.call-start = ((), (), s32[]{:S(2)}) async-start(), calls=%async_computation.11 | async-start | bytes 3145728 | tf_op jit(solution)/shard_map/psum | solution.py:101
  655.1 138.8 %reduce-scatter.25.cloned.1.call-start = ((), (), s32[]{:S(2)}) async-start(), calls=%async_computation.19 | async-start | bytes 884736
  656.8 6.5 copy-start.5
  656.8 180.6 %reduce-scatter.23.cloned.1.call-start = ((), (), s32[]{:S(2)}) async-start(), calls=%async_computation.18 | async-start | bytes 2211840
  705.3 41.6 %copy-start.32 = (bf16[24,8,4,256]{3,1,2,0:T(8,128)(2,1)}, bf16[24,8,4,256]{3,1,2,0:T(8,128)(2,1)S(1)}, u32[]{:S(2)}) copy-start(bf16[24,8,4,256]{3,1,2,0:T(8,128)(2,1)S(1)} %copy.85) | copy-start | bytes 1179652
  755.1 205.6 %all-reduce.13.cloned.1.call-start = ((), (), s32[]{:S(2)}) async-start(), calls=%async_computation.13 | async-start | bytes 6291456 | tf_op jit(solution)/shard_map/psum | solution.py:197
  760.3 6.0 copy-start.7
  760.3 6.0 copy-start.44
  760.3 6.0 copy-start.50
  760.3 245.8 %reduce-scatter.17.cloned.1.call-start = ((), (), s32[]{:S(2)}) async-start(), calls=%async_computation.15 | async-start | bytes 2654208 | tf_op jit(solution)/shard_map/reduce_scatter | solution.py:209
  766.2 4.6 copy-start.54
  766.2 286.1 %reduce-scatter.15.cloned.1.call-start = ((), (), s32[]{:S(2)}) async-start(), calls=%async_computation.14 | async-start | bytes 2654208 | tf_op jit(solution)/shard_map/reduce_scatter | solution.py:208
  772.6 22.9 %copy-start.29 = (bf16[4,256,192]{1,0,2:T(4,128)(2,1)S(1)}, bf16[4,256,192]{1,0,2:T(4,128)(2,1)}, u32[]{:S(2)}) copy-start(bf16[4,256,192]{1,0,2:T(4,128)(2,1)} %copy-done.28) | copy-start | bytes 1179652
  774.1 186.7 %copy-start.2 = (f32[4,256,767]{2,1,0:T(8,128)S(1)}, f32[4,256,767]{2,1,0:T(8,128)}, u32[]{:S(2)}) copy-start(f32[4,256,767]{2,1,0:T(8,128)} %copy-done.1) | copy-start | bytes 9424900
  774.1 186.7 %copy-start.41 = (f32[1024]{0:T(1024)S(1)}, f32[1024]{0:T(1024)}, u32[]{:S(2)}) copy-start(f32[1024]{0:T(1024)} %copy-done.40) | copy-start | bytes 12292
  774.1 186.7 %copy-start.46 = (f32[768]{0:T(1024)S(1)}, f32[768]{0:T(1024)}, u32[]{:S(2)}) copy-start(f32[768]{0:T(1024)} %param.15) | copy-start | bytes 9220
  960.8 3.1 copy-start.11
  960.8 3.1 copy-start.16
  960.8 4.1 copy-start.20
  966.7 2.5 copy-start.51
  966.7 2.5 copy-start.52
  966.8 2.5 copy-start.53
  966.8 2.5 copy-start.57
  (19 other events, 28.0 us)
Sparse Core Ops, SparseCore 0:
  33.1 21.6 all-gather.6
  56.4 19.7 all-gather.4
  88.2 121.0 all-reduce.6
  231.4 120.0 all-reduce.10
  509.4 36.8 reduce-scatter.18
  648.8 36.3 reduce-scatter.20
  687.6 68.9 all-reduce.8
  759.7 34.0 reduce-scatter.24
  797.3 40.1 reduce-scatter.22
  839.7 121.0 all-reduce.12
  964.7 41.4 reduce-scatter.16
  1009.9 42.3 reduce-scatter.14
Sparse Core Ops, SparseCore 1:
  90.5 23.8 all-gather.8
  116.1 23.8 all-gather.10
where the time goes:
time: 1070 us; the launch traced here: 1060 us
  waiting for transfers between devices  472 us (44%)
  local copies, waits for them, and re-layouts  400 us (37%)
  matrix products  69.9 us (7%)
  blocking collectives  50.5 us (5%)
  other arithmetic  48.4 us (5%)
  between operations  16.9 us (2%)
    unnamed x161, local copies, waits for them, and re-layouts  384 us
    psum x1, waiting for transfers between devices, shards(): first_grad = lax.psum(first_part, 'tp')  121 us
    psum x1, waiting for transfers between devices, shards(): second_grad = lax.psum(second_term, 'tp')  119 us
    psum x1, waiting for transfers between devices, shards(): branch = lax.psum(exit_term, 'tp') + exit_bias  109 us
    unnamed x18, waiting for transfers between devices  58 us
    reduce_scatter x1, waiting for transfers between devices, shards(): lax.psum_scatter(hidden_weight_grad, ('shard', 'ctx'), scatter_dimension=...  46.2 us
    psum x1, blocking collectives, shards(): lax.psum((first_gain_grad, entry_bias_grad, exit_bias_grad, second_gain_g...  25 us
  transfers between devices with their start and end apart: 14, of which 8 were waited for; matrix products, arithmetic and copies ran while one was open for 30% of the time, Pallas kernels for 0%

commit v1 on v0

--- a/solution.py
+++ b/solution.py
@@ -125,7 +125,25 @@
         "rd,rf->df", second_normed, hidden_grad, preferred_element_type=single
     )
     second_term = jnp.einsum("rf,df->rd", hidden_grad, full_hidden, preferred_element_type=single)
-    second_grad = lax.psum(second_term, "tp")
+
+    def _connect_frames(base_x):
+        along_axis = "tp"
+        k_all = lax.axis_size(along_axis)
+
+        def view_halves(parts_out, mid_arr):
+            if mid_arr >= k_all:
+                return parts_out
+            return view_halves(
+                parts_out
+                + lax.ppermute(
+                    parts_out, axis_name=along_axis, perm=[(s, s ^ mid_arr) for s in range(k_all)]
+                ),
+                2 * mid_arr,
+            )
+
+        return view_halves(base_x, 1)
+
+    second_grad = _connect_frames(second_term)
     second_gain_grad = jnp.sum(second_grad * second_unit, 0)
     second_scaled = second_grad * second_gain
     middle_grad = cot_full + second_inverse * (

time: 1070 us -> 1150 us (1.075)
  waiting for transfers between devices: 472 us -> 560 us
    ppermute x0 -> x2, waiting for transfers between devices: none -> 205 us  [view_halves(): lax.ppermute(parts_out, axis_name=along_axis, perm=[(s, s ^ mid_arr) for...]
    psum x1 -> x0, waiting for transfers between devices: 119 us -> none  [shards(): second_grad = lax.psum(second_term, 'tp')]
    unnamed x18 -> x17, waiting for transfers between devices: 58 us -> 58.8 us
  transfers between devices with their start and end apart: 14 -> 15, of which waited for: 8 -> 9; matrix products, arithmetic and copies ran while one was open for 30% -> 28% of each run, Pallas kernels for 0% -> 0%
where the time goes in v1:
time: 1150 us; the launch traced here: 1140 us
  waiting for transfers between devices  560 us (49%)
  local copies, waits for them, and re-layouts  398 us (35%)
  matrix products  67.9 us (6%)
  blocking collectives  50.5 us (4%)
  other arithmetic  46.9 us (4%)
  between operations  16.6 us (1%)
    unnamed x161, local copies, waits for them, and re-layouts  382 us
    ppermute x2, waiting for transfers between devices, view_halves(): lax.ppermute(parts_out, axis_name=along_axis, perm=[(s, s ^ mid_arr) for...  205 us
    psum x1, waiting for transfers between devices, shards(): first_grad = lax.psum(first_part, 'tp')  122 us
    psum x1, waiting for transfers between devices, shards(): branch = lax.psum(exit_term, 'tp') + exit_bias  109 us
    unnamed x17, waiting for transfers between devices  58.8 us
    reduce_scatter x1, waiting for transfers between devices, shards(): lax.psum_scatter(hidden_weight_grad, ('shard', 'ctx'), scatter_dimension=...  46.3 us
    psum x1, blocking collectives, shards(): lax.psum((first_gain_grad, entry_bias_grad, exit_bias_grad, second_gain_g...  25 us
  transfers between devices with their start and end apart: 15, of which 9 were waited for; matrix products, arithmetic and copies ran while one was open for 28% of the time, Pallas kernels for 0%

profile of v1, /device:TPU:0, one launch (start us, length us, event | category | flops | bytes accessed | tf_op | source)
XLA Modules:
  0.0 1142.6 jit_solution(313880302754473780)
XLA Ops:
  8.1 2.3 convert_reduce_fusion.5
  10.3 2.9 copy.52
  14.5 13.1 %all_gather.24 = bf16[3,768,192]{2,1,0:T(8,128)(2,1)S(1)} all-gather(bf16[3,96,192]{2,1,0:T(8,128)(2,1)S(1)} %copy-done.38), channel_id=1, replica_groups=mesh['shard'=2,'ctx'=4,'tp'=4] {'shard','ctx'}, dimensions={1}, use_global_device_ids=true | all-gather | bytes 995328 | tf_op jit(solution)/shard_map/all_gather | solution.py:39
  27.7 1.8 multiply_reduce_fusion.5
  33.1 2.2 fusion.20
  36.4 2.9 fusion.21
  39.2 1.5 copy.58
  42.1 12.3 %all_gather.27 = bf16[192,768]{0,1:T(8,128)(2,1)} all-gather(bf16[192,96]{0,1:T(8,128)(2,1)} %copy.58), channel_id=1, replica_groups=mesh['shard'=2,'ctx'=4,'tp'=4] {'shard','ctx'}, dimensions={1}, use_global_device_ids=true | all-gather | bytes 331776 | tf_op jit(solution)/shard_map/all_gather | solution.py:40
  56.7 2.0 copy.55
  58.6 2.9 fusion.38
  61.5 4.6 copy-done
  66.2 3.4 fusion.3
  69.5 6.7 all-gather.5.cloned.1.call-done
  76.2 1.9 copy.54
  78.1 6.6 fusion.24
  85.8 2.2 fusion.39
  89.6 4.3 copy.59
  93.9 2.2 bitcast_multiply_fusion
  97.7 2.1 convert_reduce_fusion
  99.8 109.5 %all-reduce.6.cloned.1.call-done = f32[1024,768]{1,0:T(8,128)} async-done(((f32[1024,768]{1,0:T(8,128)}), f32[1024,768]{1,0:T(8,128)}) %all-reduce.6.cloned.1.call-update) | async-done | bytes 3145744 | tf_op jit(solution)/shard_map/psum | solution.py:90
  209.3 2.2 add_reduce_fusion
  211.6 4.3 multiply_reduce_fusion.4
  215.9 5.5 fusion.33
  221.4 5.6 convert_reduce_fusion.1
  228.6 69.7 %collective-permute-done = f32[1024,768]{1,0:T(8,128)S(1)} collective-permute-done((f32[1024,768]{1,0:T(8,128)S(1)}, f32[1024,768]{1,0:T(8,128)S(1)}, u32[]{:S(2)}, u32[]{:S(2)}) %collective-permute-start) | collective-permute-done | bytes 3145760 | tf_op jit(solution)/shard_map/ppermute | solution.py:138
  298.9 1.5 collective-permute-start.1
  300.4 135.7 %collective-permute-done.1 = f32[1024,768]{1,0:T(8,128)S(1)} collective-permute-done((f32[1024,768]{1,0:T(8,128)S(1)}, f32[1024,768]{1,0:T(8,128)S(1)}, u32[]{:S(2)}, u32[]{:S(2)}) %collective-permute-start.1) | collective-permute-done | bytes 3145760 | tf_op jit(solution)/shard_map/ppermute | solution.py:138
  436.1 1.6 multiply_reduce_fusion
  437.7 1.7 fusion.36
  439.5 1.7 copy-done.10
  444.3 1.8 convolution_convert_fusion
  446.2 7.8 fusion
  454.1 3.0 fusion.2
  459.6 48.1 %copy.69 = f32[4,1024,192]{0,2,1:T(8,128)} copy(f32[4,1024,192]{1,2,0:T(8,128)S(1)} %bitcast.133) | data formatting | bytes 6291456
  507.8 84.3 %reshape.241 = f32[1024,768]{1,0:T(8,128)} reshape(f32[1024,192,4]{2,1,0:T(8,128)} %bitcast.22) | data formatting | bytes 6291456
  592.2 5.8 fusion.5
  598.0 48.1 %copy.71 = f32[4,1024,192]{0,2,1:T(8,128)} copy(f32[4,1024,192]{1,2,0:T(8,128)S(1)} %bitcast.127) | data formatting | bytes 6291456
  646.1 84.4 %reshape.243 = f32[1024,768]{1,0:T(8,128)} reshape(f32[1024,192,4]{2,1,0:T(8,128)} %bitcast.25) | data formatting | bytes 6291456
  731.8 5.1 convolution_convert_fusion.1
  737.0 1.6 convolution_bitcast_fusion
  738.7 5.3 convert_reduce_fusion.4
  745.6 29.2 %reshape.242 = bf16[256,192,4]{2,1,0:T(8,128)(2,1)} reshape(f32[256,768]{1,0:T(8,128)} %reduce-scatter.19.cloned.1.call-done) | data formatting | bytes 1179648
  774.8 12.4 %copy.70 = bf16[4,256,192]{1,0,2:T(4,128)(2,1)S(1)} copy(bf16[4,256,192]{0,2,1:T(8,128)(2,1)} %bitcast.123) | data formatting | bytes 786432
  787.3 29.3 %reshape.244 = bf16[256,192,4]{2,1,0:T(8,128)(2,1)} reshape(f32[256,768]{1,0:T(8,128)} %reduce-scatter.21.cloned.1.call-done) | data formatting | bytes 1179648
  816.6 12.2 %copy.72 = bf16[4,256,192]{1,0,2:T(4,128)(2,1)S(1)} copy(bf16[4,256,192]{0,2,1:T(8,128)(2,1)} %bitcast.124) | data formatting | bytes 786432
  831.2 3.0 copy.73
  834.2 2.9 reshape.245
  837.3 1.9 fusion.26
  839.9 2.3 add_add_fusion
  842.3 5.8 fusion.34
  848.2 4.4 fusion.32
  852.7 1.8 fusion.25
  854.6 1.5 fusion.18
  856.0 3.9 copy.66
  860.0 16.6 %reduce-scatter.25.cloned.1.call-done = f32[96,192]{1,0:T(8,128)} async-done(((f32[768,192]{1,0:T(8,128)}), f32[96,192]{1,0:T(8,128)}) %reduce-scatter.25.cloned.1.call-update) | async-done | bytes 73744
  876.6 1.6 copy.76
  879.3 40.9 %reduce-scatter.23.cloned.1.call-done = f32[96,576]{1,0:T(8,128)} async-done(((f32[768,576]{1,0:T(8,128)}), f32[96,576]{1,0:T(8,128)}) %reduce-scatter.23.cloned.1.call-update) | async-done | bytes 221200
  922.1 121.6 %all-reduce.10.cloned.1.call-done = f32[1024,768]{1,0:T(8,128)} async-done(((f32[1024,768]{1,0:T(8,128)}), f32[1024,768]{1,0:T(8,128)}) %all-reduce.10.cloned.1.call-update) | async-done | bytes 3145744 | tf_op jit(solution)/shard_map/psum | solution.py:215
  1043.7 3.0 multiply_reduce_fusion.1
  1047.8 1.5 multiply_add_fusion
  1049.9 2.2 copy.67
  1052.2 25.0 %all-reduce.1 = (f32[768]{0:T(1024)}, f32[2,192]{1,0:T(2,128)}, f32[768]{0:T(1024)}, f32[768]{0:T(1024)}, f32[768]{0:T(1024)}, /*index=5*/f32[768]{0:T(1024)}) all-reduce(f32[768]{0:T(1024)S(1)} %get-tuple-element.50, f32[2,192]{1,0:T(2,128)S(1)} %pad_maximum_fusion.2, ...), channel_id=1, replica_groups=mesh['shard'=2,'ctx'=4,'tp'=4] {'shard','ctx'}, use_global_device_ids=true, to_apply=%region_18.19 | all-reduce | flops 4224 | bytes 33792 | tf_op jit(solution)/shard_map/psum | solution.py:229
  1077.1 11.7 %reduce-scatter.17.cloned.1.call-done = f32[768,96]{0,1:T(8,128)} async-done(((f32[768,768]{0,1:T(8,128)}), f32[768,96]{0,1:T(8,128)}) %reduce-scatter.17.cloned.1.call-update) | async-done | bytes 294928 | tf_op jit(solution)/shard_map/reduce_scatter | solution.py:227
  1088.9 46.3 %reduce-scatter.15.cloned.1.call-done = f32[96,768]{1,0:T(8,128)} async-done(((f32[768,768]{1,0:T(8,128)}), f32[96,768]{1,0:T(8,128)}) %reduce-scatter.15.cloned.1.call-update) | async-done | bytes 294928 | tf_op jit(solution)/shard_map/reduce_scatter | solution.py:226
  (219 shorter events, 32.8 us)
Async XLA Ops:
  8.0 6.5 copy-start.38
  8.0 48.6 %all-gather.7.cloned.1.call-start = ((), (), s32[]{:S(2)}) async-start(), calls=%async_computation.7 | async-start | bytes 1966080 | tf_op jit(solution)/shard_map/all_gather | solution.py:58
  13.3 198.3 %copy-start.1 = (f32[4,256,767]{2,1,0:T(8,128)}, f32[4,256,767]{2,1,0:T(8,128)S(1)}, u32[]{:S(2)}) copy-start(f32[4,256,767]{2,1,0:T(8,128)S(1)} %copy.52) | copy-start | bytes 9424900
  13.3 16.2 %copy-start.45 = (f32[768]{0:T(1024)S(1)}, f32[768]{0:T(1024)}, u32[]{:S(2)}) copy-start(f32[768]{0:T(1024)} %param.15) | copy-start | bytes 9220
  14.5 15.0 %copy-start.14 = (f32[1,1024]{0,1:T(8,128)S(1)}, f32[1,1024]{0,1:T(8,128)}, u32[]{:S(2)}) copy-start(f32[1,1024]{0,1:T(8,128)} %copy.81) | copy-start | bytes 12292
  29.5 3.5 copy-start.58
  33.0 43.2 %all-gather.5.cloned.1.call-start = ((), (), s32[]{:S(2)}) async-start(), calls=%async_computation.6 | async-start | bytes 1966080 | tf_op jit(solution)/shard_map/all_gather | solution.py:59
  33.1 21.4 %copy-start.59 = (s32[4]{0:T(128)S(1)}, s32[4]{0:T(128)}, u32[]{:S(2)}) copy-start(s32[4]{0:T(128)} %param.14) | copy-start | bytes 52
  36.3 173.0 %all-reduce.6.cloned.1.call-start = ((), (), s32[]{:S(2)}) async-start(), calls=%async_computation.8 | async-start | bytes 6291456 | tf_op jit(solution)/shard_map/psum | solution.py:90
  42.1 19.4 %copy-start.25 = (bf16[4,256,3,64]{1,0,3,2:T(4,128)(2,1)}, bf16[4,256,3,64]{1,0,3,2:T(4,128)(2,1)S(1)}, u32[]{:S(2)}) copy-start(bf16[4,256,3,64]{1,0,3,2:T(4,128)(2,1)S(1)} %reshape.226) | copy-start | bytes 1179652
  58.6 2.9 copy-start.12
  61.5 4.7 copy-start
  61.5 16.6 %copy-start.36 = (f32[4,3,256]{2,1,0:T(4,128)}, f32[4,3,256]{2,1,0:T(4,128)S(1)}, u32[]{:S(2)}) copy-start(f32[4,3,256]{2,1,0:T(4,128)S(1)} %get-tuple-element.72) | copy-start | bytes 36868
  78.1 6.6 copy-start.22
  78.1 7.7 copy-start.29
  85.8 3.7 copy-start.56
  85.8 3.7 copy-start.60
  88.1 127.8 %all-gather.9.cloned.1.call-start = ((), (), s32[]{:S(2)}) async-start(), calls=%async_computation.9 | async-start | bytes 1327104 | tf_op jit(solution)/shard_map/all_gather | solution.py:41
  88.7 132.7 %all-gather.11.cloned.1.call-start = ((), (), s32[]{:S(2)}) async-start(), calls=%async_computation.10 | async-start | bytes 1327104 | tf_op jit(solution)/shard_map/all_gather | solution.py:42
  89.3 656.3 %reduce-scatter.19.cloned.1.call-start = ((), (), s32[]{:S(2)}) async-start(), calls=%async_computation.15 | async-start | bytes 3932160
  96.4 113.0 %copy-start.47 = (f32[768]{0:T(1024)S(1)}, f32[768]{0:T(1024)}, u32[]{:S(2)}) copy-start(f32[768]{0:T(1024)} %param.19) | copy-start | bytes 9220
  211.6 4.3 copy-start.48
  215.9 221.8 %copy-start.43 = (f32[1024]{0:T(1024)}, f32[1024]{0:T(1024)S(1)}, u32[]{:S(2)}) copy-start(f32[1024]{0:T(1024)S(1)} %add_rsqrt_fusion) | copy-start | bytes 12292
  215.9 5.5 copy-start.35
  215.9 5.5 copy-start.63
  221.4 5.6 copy-start.62
  228.4 71.9 %copy-start.37 = (f32[4,3,256]{2,1,0:T(4,128)S(1)}, f32[4,3,256]{2,1,0:T(4,128)}, u32[]{:S(2)}) copy-start(f32[4,3,256]{2,1,0:T(4,128)} %copy-done.36) | copy-start | bytes 36868
  228.5 71.9 %copy-start.40 = (f32[4,3,256]{2,1,0:T(4,128)S(1)}, f32[4,3,256]{2,1,0:T(4,128)}, u32[]{:S(2)}) copy-start(f32[4,3,256]{2,1,0:T(4,128)} %fusion.3) | copy-start | bytes 36868
  228.5 207.6 %copy-start.6 = (f32[1024,768]{1,0:T(8,128)S(1)}, f32[1024,768]{1,0:T(8,128)}, u32[]{:S(2)}) copy-start(f32[1024,768]{1,0:T(8,128)} %get-tuple-element.67) | copy-start | bytes 9437188
  228.5 207.6 %copy-start.49 = (f32[768]{0:T(1024)S(1)}, f32[768]{0:T(1024)}, u32[]{:S(2)}) copy-start(f32[768]{0:T(1024)} %param.20) | copy-start | bytes 9220
  228.5 69.7 %collective-permute-start = (f32[1024,768]{1,0:T(8,128)S(1)}, f32[1024,768]{1,0:T(8,128)S(1)}, u32[]{:S(2)}, u32[]{:S(2)}) collective-permute-start(f32[1024,768]{1,0:T(8,128)S(1)} %fusion.40), channel_id=1, source_target_pairs={{0,1},{1,0},{2,3},{3,2},{4,5},{5,4},{6,7},{7,6},{8,9},{9,8},{10,11... | collective-permute-start | bytes 9437192 | tf_op jit(solution)/shard_map/ppermute | solution.py:138
  298.9 137.2 %collective-permute-start.1 = (f32[1024,768]{1,0:T(8,128)S(1)}, f32[1024,768]{1,0:T(8,128)S(1)}, u32[]{:S(2)}, u32[]{:S(2)}) collective-permute-start(f32[1024,768]{1,0:T(8,128)S(1)} %add.165), channel_id=1, source_target_pairs={{0,2},{1,3},{2,0},{3,1},{4,6},{5,7},{6,4},{7,5},{8,10},{9,11},{10,... | collective-permute-start | bytes 9437192 | tf_op jit(solution)/shard_map/ppermute | solution.py:138
  300.4 137.3 %copy-start.9 = (f32[1024,767]{1,0:T(8,128)S(1)}, f32[1024,767]{1,0:T(8,128)}, u32[]{:S(2)}) copy-start(f32[1024,767]{1,0:T(8,128)} %copy-done.8) | copy-start | bytes 9424900
  441.2 3.1 copy-start.23
  444.3 9.7 slice-start
  444.3 9.7 slice-start.1
  446.1 7.9 slice-start.2
  454.0 3.0 copy-start.26
  457.1 2.6 copy-start.3
  592.1 195.2 %reduce-scatter.21.cloned.1.call-start = ((), (), s32[]{:S(2)}) async-start(), calls=%async_computation.16 | async-start | bytes 3932160
  730.5 6.5 copy-start.18
  730.5 6.5 copy-start.34
  730.5 122.2 %all-reduce.8.cloned.1.call-start = ((), (), s32[]{:S(2)}) async-start(), calls=%async_computation.11 | async-start | bytes 3145728 | tf_op jit(solution)/shard_map/psum | solution.py:101
  736.9 139.7 %reduce-scatter.25.cloned.1.call-start = ((), (), s32[]{:S(2)}) async-start(), calls=%async_computation.18 | async-start | bytes 884736
  738.6 6.5 copy-start.5
  738.6 181.6 %reduce-scatter.23.cloned.1.call-start = ((), (), s32[]{:S(2)}) async-start(), calls=%async_computation.17 | async-start | bytes 2211840
  787.3 41.6 %copy-start.31 = (bf16[24,8,4,256]{3,1,2,0:T(8,128)(2,1)}, bf16[24,8,4,256]{3,1,2,0:T(8,128)(2,1)S(1)}, u32[]{:S(2)}) copy-start(bf16[24,8,4,256]{3,1,2,0:T(8,128)(2,1)S(1)} %copy.85) | copy-start | bytes 1179652
  837.1 206.6 %all-reduce.10.cloned.1.call-start = ((), (), s32[]{:S(2)}) async-start(), calls=%async_computation.12 | async-start | bytes 6291456 | tf_op jit(solution)/shard_map/psum | solution.py:215
  842.3 6.0 copy-start.7
  842.3 6.0 copy-start.44
  842.3 6.0 copy-start.50
  842.3 246.6 %reduce-scatter.17.cloned.1.call-start = ((), (), s32[]{:S(2)}) async-start(), calls=%async_computation.14 | async-start | bytes 2654208 | tf_op jit(solution)/shard_map/reduce_scatter | solution.py:227
  848.2 4.6 copy-start.54
  848.2 287.0 %reduce-scatter.15.cloned.1.call-start = ((), (), s32[]{:S(2)}) async-start(), calls=%async_computation.13 | async-start | bytes 2654208 | tf_op jit(solution)/shard_map/reduce_scatter | solution.py:226
  854.5 23.7 %copy-start.28 = (bf16[4,256,192]{1,0,2:T(4,128)(2,1)S(1)}, bf16[4,256,192]{1,0,2:T(4,128)(2,1)}, u32[]{:S(2)}) copy-start(bf16[4,256,192]{1,0,2:T(4,128)(2,1)} %copy-done.27) | copy-start | bytes 1179652
  856.0 187.6 %copy-start.2 = (f32[4,256,767]{2,1,0:T(8,128)S(1)}, f32[4,256,767]{2,1,0:T(8,128)}, u32[]{:S(2)}) copy-start(f32[4,256,767]{2,1,0:T(8,128)} %copy-done.1) | copy-start | bytes 9424900
  856.0 187.6 %copy-start.42 = (f32[1024]{0:T(1024)S(1)}, f32[1024]{0:T(1024)}, u32[]{:S(2)}) copy-start(f32[1024]{0:T(1024)} %copy-done.41) | copy-start | bytes 12292
  856.0 187.6 %copy-start.46 = (f32[768]{0:T(1024)S(1)}, f32[768]{0:T(1024)}, u32[]{:S(2)}) copy-start(f32[768]{0:T(1024)} %param.15) | copy-start | bytes 9220
  1043.7 3.1 copy-start.11
  1043.7 3.1 copy-start.16
  1043.7 4.1 copy-start.19
  1049.6 2.5 copy-start.51
  1049.7 2.5 copy-start.52
  1049.7 2.5 copy-start.53
  (20 other events, 30.5 us)
Sparse Core Ops, SparseCore 0:
  33.1 21.6 all-gather.6
  56.4 19.7 all-gather.4
  88.2 121.0 all-reduce.5
  592.3 37.4 reduce-scatter.18
  730.6 37.4 reduce-scatter.20
  770.3 68.9 all-reduce.7
  842.5 34.0 reduce-scatter.24
  880.0 40.1 reduce-scatter.22
  922.6 121.0 all-reduce.9
  1047.4 41.4 reduce-scatter.16
  1092.8 42.3 reduce-scatter.14
Sparse Core Ops, SparseCore 1:
  90.5 23.8 all-gather.8
  116.1 23.8 all-gather.10
